TPU v7x, 32 devices: a whole 2x2x4 slice. The times are simulated.
32 devices in a mesh: seq: 8 (over y, x, core), ch: 4 (over z).
Axes of the slice: x: 2, y: 2, z: 4, core: 2. Of those that a mesh axis runs over, the one named last changes fastest.
Arguments:
- signal: bfloat16 [1024, 128, 1024], P('seq', 'ch'), may hold values from -6 to 6
- cotangent: bfloat16 [1024, 128, 1024], P('seq', 'ch'), may hold values from -6 to 6
- right_factor: bfloat16 [1024, 1024], replicated, may hold values from -0.1875 to 0.1875
- left_factor: bfloat16 [1024, 1024], replicated, may hold values from -0.1875 to 0.1875
- right_blocks: int32 [8, 8], replicated, may hold values 0 or 1
- left_blocks: int32 [8, 8], replicated, may hold values 0 or 1
Outputs:
- mixed: bfloat16 [1024, 128, 1024], P('seq', 'ch')
- grad_signal: bfloat16 [1024, 128, 1024], P('seq', 'ch')
- grad_right: float32 [1024, 1024], P('seq', 'ch')
- grad_left: float32 [1024, 1024], P('seq', 'ch')
All inputs are finite; a program needn't handle non-finite values.
Results may differ from a plain program's by a relative error of at most 0.0051.
Values may be sent and summed in bfloat16 or wider, within the bound.
A program may use at most 192 MiB of HBM per device.

v0:
```python
import math

import jax
import jax.numpy as jnp
from jax import lax
from jax.sharding import PartitionSpec as P


def expand(blocks, width):
    tile = width // blocks.shape[0]
    return jnp.repeat(jnp.repeat(blocks, tile, axis=0), tile, axis=1)


def to_columns(rows, peers):
    rows_here, chans, width_two = rows.shape
    piece = width_two // peers
    arranged = rows.reshape(rows_here, chans, peers, piece).transpose(0, 2, 1, 3)
    return arranged.reshape(rows_here, peers, chans * piece)


def to_rows(received, chans):
    rows_here, peers, wide = received.shape
    piece = wide // chans
    arranged = received.reshape(rows_here, peers, chans, piece).transpose(0, 2, 1, 3)
    return arranged.reshape(rows_here, chans, peers * piece)


def shards(signal, cotangent, right_factor, left_factor, right_blocks, left_blocks):
    rows_here, chans, width_two = signal.shape
    width_one = left_factor.shape[0]
    peers = lax.axis_size("seq")
    right_mask = expand(right_blocks, width_two).astype(jnp.bfloat16)
    left_mask = expand(left_blocks, width_one).astype(jnp.bfloat16)
    right_eff = right_factor * right_mask
    left_eff = left_factor * left_mask
    flat_signal = signal.reshape(rows_here * chans, width_two)
    first_rows = jnp.dot(flat_signal, right_eff.T, preferred_element_type=jnp.float32)
    first_rows = to_columns(
        first_rows.astype(jnp.bfloat16).reshape(rows_here, chans, width_two), peers
    )
    sig_f = signal.astype(jnp.float32)
    gate = jax.nn.sigmoid(sig_f)
    swish = sig_f * gate
    cot_f = cotangent.astype(jnp.float32)
    grad_rows = to_columns((cot_f * swish).astype(jnp.bfloat16), peers)
    z_cols = lax.all_to_all(first_rows, "seq", split_axis=1, concat_axis=0, tiled=True)
    flat_cols = z_cols.reshape(width_one, z_cols.shape[2])
    result = jnp.dot(left_eff, flat_cols, preferred_element_type=jnp.float32)
    y_cols = result.astype(jnp.bfloat16).reshape(width_one, 1, z_cols.shape[2])
    y_back = lax.all_to_all(y_cols, "seq", split_axis=0, concat_axis=1, tiled=True)
    dy_cols = lax.all_to_all(grad_rows, "seq", split_axis=1, concat_axis=0, tiled=True)
    flat_cols = dy_cols.reshape(width_one, dy_cols.shape[2])
    result = lax.dot_general(
        left_eff, flat_cols, (((0,), (0,)), ((), ())), preferred_element_type=jnp.float32
    )
    dz_cols = result.astype(jnp.bfloat16).reshape(width_one, 1, dy_cols.shape[2])
    dz_back = lax.all_to_all(dz_cols, "seq", split_axis=0, concat_axis=1, tiled=True)
    y_rows = to_rows(y_back, chans)
    dz_rows = to_rows(dz_back, chans)
    y_f = y_rows.astype(jnp.float32)
    mixed = (sig_f + y_f * swish).astype(jnp.bfloat16)
    dz_flat = dz_rows.reshape(rows_here * chans, width_two)
    back = jnp.dot(dz_flat, right_eff, preferred_element_type=jnp.float32).reshape(
        rows_here, chans, width_two
    )
    dswish = gate * (1.0 + sig_f * (1.0 - gate))
    grad_signal = (cot_f * (1.0 + y_f * dswish) + back).astype(jnp.bfloat16)
    wide = z_cols.shape[2]
    z_flat = z_cols.reshape(width_one, wide)
    dy_flat = dy_cols.reshape(width_one, wide)
    left_term = lax.dot_general(
        dy_flat, z_flat, (((1,), (1,)), ((), ())), preferred_element_type=jnp.float32
    )
    right_term = lax.dot_general(
        dz_flat, flat_signal, (((0,), (0,)), ((), ())), preferred_element_type=jnp.float32
    )
    total_chans = chans * lax.axis_size("ch")
    right_term = right_term * right_mask.astype(jnp.float32) / math.sqrt(width_one * total_chans)
    left_term = left_term * left_mask.astype(jnp.float32) / math.sqrt(width_two * total_chans)
    partial_value = (
        lax.psum_scatter(right_term, "seq", scatter_dimension=0, tiled=True),
        lax.psum_scatter(left_term, "seq", scatter_dimension=0, tiled=True),
    )
    grad_right, grad_left = (
        lax.psum_scatter(partial_value[0], "ch", scatter_dimension=1, tiled=True),
        lax.psum_scatter(partial_value[1], "ch", scatter_dimension=1, tiled=True),
    )
    return (mixed, grad_signal, grad_right, grad_left)


def solution(mesh):
    return jax.shard_map(
        shards,
        mesh=mesh,
        in_specs=(P("seq", "ch", None), P("seq", "ch", None), P(), P(), P(), P()),
        out_specs=(P("seq", "ch", None), P("seq", "ch", None), P("seq", "ch"), P("seq", "ch")),
        check_vma=False,
    )
```

profile of v0, /device:TPU:0, one launch (start us, length us, event | category | flops | bytes accessed | tf_op | source)
XLA Modules:
  0.0 901.5 jit_solution(9334376529335361705)
XLA Ops:
  12.2 14.0 %convert_bitcast_fusion.3 = bf16[4096,1024]{0,1:T(8,128)(2,1)} fusion(bf16[4096,1024]{1,0:T(8,128)(2,1)} %bitcast.103, bf16[1024,1024]{1,0:T(8,128)(2,1)} %param.8, bf16[128,8,8,128]{3,2,1,0:T(8,128)(2,1)S(1)} %bitcast.105), kind=kOutput, calls=%fused_computation.24 | convolution fusion | flops 8595177472 | bytes 20971520 | tf_op jit(solution)/shard_map/dot_general | solution.py:37
  26.1 11.9 %copy.69 = bf16[4096,1024]{1,0:T(8,128)(2,1)} copy(bf16[4096,1024]{0,1:T(8,128)(2,1)} %convert_bitcast_fusion.3) | data formatting | bytes 16777216 | tf_op jit(solution)/shard_map/convert_element_type | solution.py:39
  54.9 12.6 %copy.70 = bf16[128,8,32,128]{0,3,2,1:T(8,128)(2,1)} copy(bf16[128,8,32,128]{3,1,2,0:T(8,128)(2,1)} %bitcast_bitcast_fusion) | data formatting | bytes 16777216 | tf_op jit(solution)/shard_map/transpose | solution.py:17
  73.1 94.4 %all-to-all-done = bf16[128,8,4096]{0,2,1:T(8,128)(2,1)} async-done(((bf16[128,8,4096]{0,2,1:T(8,128)(2,1)}), bf16[128,8,4096]{0,2,1:T(8,128)(2,1)}, u32[]{:S(2)}, u32[]{:S(2)}) %all-to-all-start) | async-done | bytes 8388640 | tf_op jit(solution)/shard_map/all_to_all | solution.py:46
  167.5 12.0 %copy.71 = bf16[8,128,1,4096]{3,1,0,2:T(8,128)(2,1)} copy(bf16[8,128,1,4096]{1,3,0,2:T(8,128)(2,1)} %bitcast.7) | data formatting | bytes 16777216 | tf_op jit(solution)/shard_map/all_to_all | solution.py:46
  182.5 13.9 %convert_bitcast_fusion.2 = bf16[1024,1,4096]{2,0,1:T(8,128)(2,1)} fusion(bf16[1024,4096]{1,0:T(8,128)(2,1)} %bitcast.98, bf16[1024,1024]{1,0:T(8,128)(2,1)} %param.9, bf16[128,8,8,128]{3,2,1,0:T(8,128)(2,1)S(1)} %bitcast.108), kind=kOutput, calls=%fused_computation.23 | convolution fusion | flops 8595177472 | bytes 20971520 | tf_op jit(solution)/shard_map/dot_general | solution.py:48
  219.2 100.1 %all_to_all.57 = bf16[8,2,262144]{2,1,0:T(2,128)(2,1)} all-to-all(bf16[8,2,262144]{2,1,0:T(2,128)(2,1)} %reshape.71), channel_id=1, replica_groups=mesh['seq'=8,'ch'=4] {'seq'}, dimensions={0} | all-to-all | bytes 16777216 | tf_op jit(solution)/shard_map/all_to_all | solution.py:50
  319.3 13.3 %reshape.72 = bf16[1024,1,4096]{2,1,0:T(2,128)(2,1)} reshape(bf16[8,2,262144]{2,1,0:T(2,128)(2,1)} %all_to_all.57) | data formatting | bytes 16777216
  332.6 16.8 %copy.73 = bf16[1024,1,4096]{2,0,1:T(8,128)(2,1)} copy(bf16[1024,1,4096]{2,1,0:T(2,128)(2,1)} %reshape.72) | data formatting | bytes 16777216 | tf_op jit(solution)/shard_map/all_to_all | solution.py:50
  349.4 11.4 %convert_bitcast_fusion = f32[128,8,1,4096]{3,0,1,2:T(8,128)} fusion(bf16[8,128,1,4096]{3,1,0,2:T(8,128)(2,1)} %bitcast.89), kind=kLoop, calls=%fused_computation.17 | loop fusion | flops 4194304 | bytes 25165824 | tf_op jit(solution)/shard_map/convert_element_type | solution.py:60
  360.8 17.4 %copy.74 = f32[128,8,1,4096]{0,3,1,2:T(8,128)} copy(f32[128,8,1,4096]{3,0,1,2:T(8,128)} %convert_bitcast_fusion) | data formatting | bytes 33554432 | tf_op jit(solution)/shard_map/convert_element_type | solution.py:60
  378.2 17.5 %copy.75 = f32[128,32,8,128]{3,2,0,1:T(8,128)} copy(f32[128,32,8,128]{0,3,1,2:T(8,128)} %bitcast.88) | data formatting | bytes 33554432 | tf_op jit(solution)/shard_map/convert_element_type | solution.py:60
  395.7 18.0 %reshape.67 = f32[128,32,1024]{2,0,1:T(8,128)} reshape(f32[128,32,8,128]{3,2,0,1:T(8,128)} %copy.75) | data formatting | bytes 33554432 | tf_op jit(solution)/shard_map/convert_element_type | solution.py:60
  413.7 22.3 %fusion.2 = (bf16[128,32,1024]{2,0,1:T(8,128)(2,1)}, bf16[128,32,1024]{2,0,1:T(8,128)(2,1)}) fusion(bf16[128,32,1024]{2,1,0:T(8,128)(2,1)} %param.7, bf16[128,32,1024]{2,1,0:T(8,128)(2,1)} %param.6, f32[128,32,1024]{2,0,1:T(8,128)} %reshape.67), kind=kLoop, calls=%fused_computation.8 | loop fusion | flops 46137344 | bytes 50331648 | tf_op jit(solution)/shard_map/convert_element_type | solution.py:45
  444.8 12.4 %copy.77 = bf16[128,32,8,128]{0,3,1,2:T(8,128)(2,1)} copy(bf16[128,32,8,128]{3,2,0,1:T(8,128)(2,1)} %bitcast.94) | data formatting | bytes 16777216 | tf_op jit(solution)/shard_map/reshape | solution.py:17
  457.1 99.7 %all_to_all.58 = bf16[128,8,4096]{0,2,1:T(8,128)(2,1)} all-to-all(bf16[128,8,4096]{0,2,1:T(8,128)(2,1)} %bitcast.95), channel_id=1, replica_groups=mesh['seq'=8,'ch'=4] {'seq'}, dimensions={1} | all-to-all | bytes 16777216 | tf_op jit(solution)/shard_map/all_to_all | solution.py:51
  556.8 12.0 %copy.78 = bf16[8,128,1,4096]{3,1,0,2:T(8,128)(2,1)} copy(bf16[8,128,1,4096]{1,3,0,2:T(8,128)(2,1)} %bitcast.96) | data formatting | bytes 16777216 | tf_op jit(solution)/shard_map/all_to_all | solution.py:51
  568.8 14.3 %convert_bitcast_fusion.1 = bf16[1024,1,4096]{2,0,1:T(8,128)(2,1)} fusion(bf16[1024,4096]{1,0:T(8,128)(2,1)} %bitcast.100, bf16[1024,1024]{1,0:T(8,128)(2,1)} %param.9, bf16[128,8,8,128]{3,2,1,0:T(8,128)(2,1)S(1)} %bitcast.109), kind=kOutput, calls=%fused_computation.22 | convolution fusion | flops 8595177472 | bytes 20971520 | tf_op jit(solution)/shard_map/dot_general | solution.py:53
  594.2 11.2 %reshape.73 = bf16[8,2,262144]{2,1,0:T(2,128)(2,1)} reshape(bf16[1024,4096]{1,0:T(8,128)(2,1)} %reduce.1) | data formatting | bytes 16777216
  610.4 15.6 %multiply_multiply_fusion = f32[1024,1024]{1,0:T(8,128)} fusion(bf16[1024,4096]{1,0:T(8,128)(2,1)} %bitcast.101, bf16[1024,4096]{1,0:T(8,128)(2,1)} %bitcast.99, bf16[128,8,8,128]{3,2,1,0:T(8,128)(2,1)S(1)} %bitcast.110), kind=kOutput, calls=%fused_computation.25 | convolution fusion | flops 8593080320 | bytes 23068672 | tf_op jit(solution)/shard_map/dot_general | solution.py:71
  626.0 95.2 %all-to-all-done.3 = bf16[8,2,262144]{2,1,0:T(2,128)(2,1)} async-done(((bf16[8,2,262144]{2,1,0:T(2,128)(2,1)}), bf16[8,2,262144]{2,1,0:T(2,128)(2,1)}, u32[]{:S(2)}, u32[]{:S(2)}) %all-to-all-start.3) | async-done | bytes 8388640 | tf_op jit(solution)/shard_map/all_to_all | solution.py:57
  721.2 13.3 %reshape.74 = bf16[1024,1,4096]{2,1,0:T(2,128)(2,1)} reshape(bf16[8,2,262144]{2,1,0:T(2,128)(2,1)} %all-to-all-done.3) | data formatting | bytes 16777216
  734.5 16.8 %copy.85 = bf16[1024,1,4096]{2,0,1:T(8,128)(2,1)} copy(bf16[1024,1,4096]{2,1,0:T(2,128)(2,1)} %reshape.74) | data formatting | bytes 16777216
  751.4 11.9 %copy.80 = bf16[128,8,1,4096]{0,3,1,2:T(8,128)(2,1)} copy(bf16[128,8,1,4096]{3,0,1,2:T(8,128)(2,1)} %bitcast.90) | data formatting | bytes 16777216 | tf_op jit(solution)/shard_map/all_to_all | solution.py:57
  763.3 12.6 %copy.82 = bf16[128,32,8,128]{3,2,1,0:T(8,128)(2,1)} copy(bf16[128,32,8,128]{0,3,1,2:T(8,128)(2,1)} %bitcast.86) | data formatting | bytes 16777216 | tf_op jit(solution)/shard_map/transpose | solution.py:24
  775.9 15.2 %multiply_multiply_fusion.1 = f32[1024,1024]{1,0:T(8,128)} fusion(bf16[4096,1024]{1,0:T(8,128)(2,1)} %bitcast.104, bf16[512,8,8,128]{3,2,1,0:T(8,128)(2,1)} %bitcast.102, bf16[128,8,8,128]{3,2,1,0:T(8,128)(2,1)S(1)} %bitcast.106), kind=kOutput, calls=%fused_computation.26 | convolution fusion | flops 8593080320 | bytes 23068672 | tf_op jit(solution)/shard_map/dot_general | solution.py:74
  792.0 11.8 %copy.83 = bf16[128,32,1024]{2,1,0:T(8,128)(2,1)} copy(bf16[128,32,1024]{2,0,1:T(8,128)(2,1)} %get-tuple-element.29) | data formatting | bytes 16777216
  803.8 12.5 %copy.81 = bf16[128,32,8,128]{3,2,0,1:T(8,128)(2,1)} copy(bf16[128,32,8,128]{0,3,1,2:T(8,128)(2,1)} %bitcast.87) | data formatting | bytes 16777216 | tf_op jit(solution)/shard_map/transpose | solution.py:24
  816.3 13.4 %dot_general.23 = bf16[128,32,1024]{2,0,1:T(8,128)(2,1)} reshape(bf16[128,32,8,128]{3,2,0,1:T(8,128)(2,1)} %copy.81) | data formatting | bytes 16777216 | tf_op jit(solution)/shard_map/dot_general | solution.py:63
  829.7 13.0 %reduce-scatter.5.cloned.1.call-done = f32[128,1024]{1,0:T(8,128)} async-done(((f32[1024,1024]{1,0:T(8,128)}), f32[128,1024]{1,0:T(8,128)}) %reduce-scatter.5.cloned.1.call-update) | async-done | bytes 524304 | tf_op jit(solution)/shard_map/reduce_scatter | solution.py:81
  842.7 40.5 %fusion.1 = bf16[128,32,1024]{2,0,1:T(8,128)(2,1)} fusion(f32[128,32,1024]{2,0,1:T(8,128)} %reshape.67, bf16[128,32,1024]{2,0,1:T(8,128)(2,1)} %dot_general.23, bf16[128,32,1024]{2,1,0:T(8,128)(2,1)} %param.7, bf16[128,32,1024]{2,1,0:T(8,128)(2,1)} %param.6, bf16[1024,1024]{1,0:T(8,128)(2,1)} %param.8, bf16[128,8,8,128]{3,2,1,0:T(8,128)(2,1)S(1)} %bitcast.107), kind=kOutput, calls=%fused_computation.7 | convolution fusion | flops 8649703424 | bytes 54525952 | tf_op jit(solution)/shard_map/dot_general | solution.py:63
  883.2 11.5 %copy.84 = bf16[128,32,1024]{2,1,0:T(8,128)(2,1)} copy(bf16[128,32,1024]{2,0,1:T(8,128)(2,1)} %fusion.1) | data formatting | bytes 16777216
  (32 shorter events, 79.1 us)
Async XLA Ops:
  10.8 1.3 copy-start
  67.5 5.6 copy-start.2
  67.5 100.0 %all-to-all-start = ((bf16[128,8,4096]{0,2,1:T(8,128)(2,1)}), bf16[128,8,4096]{0,2,1:T(8,128)(2,1)}, u32[]{:S(2)}, u32[]{:S(2)}) async-start(bf16[128,8,4096]{0,2,1:T(8,128)(2,1)} %bitcast.91), calls=%async_computation | async-start | bytes 16777216 | tf_op jit(solution)/shard_map/all_to_all | solution.py:46
  605.4 115.9 %all-to-all-start.3 = ((bf16[8,2,262144]{2,1,0:T(2,128)(2,1)}), bf16[8,2,262144]{2,1,0:T(2,128)(2,1)}, u32[]{:S(2)}, u32[]{:S(2)}) async-start(bf16[8,2,262144]{2,1,0:T(2,128)(2,1)} %reshape.73), calls=%async_computation.3 | async-start | bytes 16777216 | tf_op jit(solution)/shard_map/all_to_all | solution.py:57
  610.3 180.8 %reduce-scatter.9.cloned.1.call-start = ((), (), s32[]{:S(2)}) async-start(), calls=%async_computation.10 | async-start | bytes 4718592 | tf_op jit(solution)/shard_map/reduce_scatter | solution.py:82
  626.0 216.7 %reduce-scatter.5.cloned.1.call-start = ((), (), s32[]{:S(2)}) async-start(), calls=%async_computation.8 | async-start | bytes 4718592 | tf_op jit(solution)/shard_map/reduce_scatter | solution.py:81
  763.3 12.6 %copy-start.1 = (bf16[1024,8,128]{2,1,0:T(8,128)(2,1)S(1)}, bf16[1024,8,128]{2,1,0:T(8,128)(2,1)}, u32[]{:S(2)}) copy-start(bf16[1024,8,128]{2,1,0:T(8,128)(2,1)} %copy-done) | copy-start | bytes 6291460
  791.1 103.7 %reduce-scatter.11.cloned.1.call-start = ((), (), s32[]{:S(2)}) async-start(), calls=%async_computation.11 | async-start | bytes 655360 | tf_op jit(solution)/shard_map/reduce_scatter | solution.py:86
  791.8 102.9 %reduce-scatter.7.cloned.1.call-start = ((), (), s32[]{:S(2)}) async-start(), calls=%async_computation.9 | async-start | bytes 655360 | tf_op jit(solution)/shard_map/reduce_scatter | solution.py:85
Sparse Core Ops, SparseCore 0:
  626.1 94.0 reduce-scatter.8
  791.2 51.4 reduce-scatter.4
  845.5 21.6 reduce-scatter.10
  869.9 19.8 reduce-scatter.6
where the time goes:
time: 913 us; the launch traced here: 902 us
  local copies, waits for them, and re-layouts  303 us (33%)
  waiting for transfers between devices  203 us (22%)
  blocking collectives  200 us (22%)
  matrix products  113 us (12%)
  other arithmetic  56.6 us (6%)
  between operations  14.1 us (2%)
  starting transfers between devices  10.9 us (1%)
    unnamed x15, local copies, waits for them, and re-layouts  108 us
    all_to_all x1, blocking collectives, shards(): lax.all_to_all(y_cols, 'seq', split_axis=0, concat_axis=1, tiled=True)  100 us
    all_to_all x1, blocking collectives, shards(): lax.all_to_all(grad_rows, 'seq', split_axis=1, concat_axis=0, tiled=True)  99.7 us
    all_to_all x1, waiting for transfers between devices, shards(): lax.all_to_all(dz_cols, 'seq', split_axis=0, concat_axis=1, tiled=True)  95.2 us
    all_to_all x1, waiting for transfers between devices, shards(): lax.all_to_all(first_rows, 'seq', split_axis=1, concat_axis=0, tiled=True)  94.4 us
    convert_element_type x3, local copies, waits for them, and re-layouts, shards(): y_f = y_rows.astype(jnp.float32)  52.9 us
    dot_general x1, matrix products, shards(): jnp.dot(dz_flat, right_eff, preferred_element_type=jnp.float32)  40.5 us
    transpose x2, local copies, waits for them, and re-layouts, to_rows(): received.reshape(rows_here, peers, chans, piece).transpose(0, 2, 1, 3)  25.1 us
  transfers between devices with their start and end apart: 6, of which 3 were waited for; matrix products, arithmetic and copies ran while one was open for 19% of the time, Pallas kernels for 0%

commit v1 on v0

--- a/solution.py
+++ b/solution.py
@@ -1,8 +1,11 @@
+import functools
 import math
 
 import jax
 import jax.numpy as jnp
 from jax import lax
+from jax.experimental import pallas as pl
+from jax.experimental.pallas import tpu as pltpu
 from jax.sharding import PartitionSpec as P
 
 
@@ -25,7 +28,7 @@
     return arranged.reshape(rows_here, chans, peers * piece)
 
 
-def shards(signal, cotangent, right_factor, left_factor, right_blocks, left_blocks):
+def shards_by_column(signal, cotangent, right_factor, left_factor, right_blocks, left_blocks):
     rows_here, chans, width_two = signal.shape
     width_one = left_factor.shape[0]
     peers = lax.axis_size("seq")
@@ -88,6 +91,235 @@
     return (mixed, grad_signal, grad_right, grad_left)
 
 
+def mix_kernel(
+    peers, parts, xt, ct, right, left, left_t, mt, gt, grad_r, grad_l,
+    xbuf, cbuf, zbuf, dybuf, dzbuf, send_sem, recv_sem, local_sem,
+):
+    me = lax.axis_index("seq")
+    column = lax.axis_index("ch")
+    rows = xt.shape[1]
+    width = xt.shape[2]
+    order = left.shape[0]
+    tile = 256
+
+    def own_rows(who):
+        return pl.ds(pl.multiple_of(who * rows, rows), rows)
+
+    def far(kind, part, source, target, who):
+        return pltpu.make_async_remote_copy(
+            src_ref=source,
+            dst_ref=target,
+            send_sem=send_sem.at[kind, part, who],
+            recv_sem=recv_sem.at[kind, part, me],
+            device_id=(who, column),
+            device_id_type=pl.DeviceIdType.MESH,
+        )
+
+    def arrived(kind, part, source, target, who):
+        return pltpu.make_async_remote_copy(
+            src_ref=source,
+            dst_ref=target,
+            send_sem=send_sem.at[kind, part, who],
+            recv_sem=recv_sem.at[kind, part, who],
+            device_id=(who, column),
+            device_id_type=pl.DeviceIdType.MESH,
+        )
+
+    def each_peer(action):
+        @pl.loop(1, peers)
+        def _(step):
+            action(lax.rem(me + step, peers))
+
+    barrier = pltpu.get_barrier_semaphore()
+
+    def greet(who):
+        pl.semaphore_signal(
+            barrier, inc=1, device_id=(who, column), device_id_type=pl.DeviceIdType.MESH
+        )
+
+    each_peer(greet)
+    pl.semaphore_wait(barrier, peers - 1)
+
+    inputs = ((0, xt, xbuf), (1, ct, cbuf))
+    outputs = ((2, mt, xbuf), (3, gt, cbuf))
+
+    def send_in(part):
+        def one(who):
+            for kind, source, held in inputs:
+                far(kind, part, source.at[part * peers + who], held.at[part, own_rows(me)], who).start()
+
+        each_peer(one)
+        for kind, source, held in inputs:
+            pltpu.make_async_copy(
+                source.at[part * peers + me], held.at[part, own_rows(me)], local_sem.at[kind, part]
+            ).start()
+
+    def wait_in(part):
+        def one(who):
+            for kind, source, held in inputs:
+                arrived(
+                    kind, part, source.at[part * peers + who], held.at[part, own_rows(who)], who
+                ).wait_recv()
+
+        each_peer(one)
+        for kind, source, held in inputs:
+            pltpu.make_async_copy(
+                source.at[part * peers + me], held.at[part, own_rows(me)], local_sem.at[kind, part]
+            ).wait()
+
+    def wait_in_sent(part):
+        def one(who):
+            for kind, source, held in inputs:
+                far(kind, part, source.at[part * peers + who], held.at[part, own_rows(me)], who).wait_send()
+
+        each_peer(one)
+
+    def send_out(part):
+        def one(who):
+            for kind, target, held in outputs:
+                far(kind, part, held.at[part, own_rows(who)], target.at[part * peers + me], who).start()
+
+        each_peer(one)
+        for kind, target, held in outputs:
+            pltpu.make_async_copy(
+                held.at[part, own_rows(me)], target.at[part * peers + me], local_sem.at[kind, part]
+            ).start()
+
+    def wait_out(part):
+        def one(who):
+            for kind, target, held in outputs:
+                arrived(
+                    kind, part, held.at[part, own_rows(who)], target.at[part * peers + who], who
+                ).wait_recv()
+                far(kind, part, held.at[part, own_rows(who)], target.at[part * peers + me], who).wait_send()
+
+        each_peer(one)
+        for kind, target, held in outputs:
+            pltpu.make_async_copy(
+                held.at[part, own_rows(me)], target.at[part * peers + me], local_sem.at[kind, part]
+            ).wait()
+
+    def at(step):
+        return pl.ds(pl.multiple_of(step * tile, tile), tile)
+
+    def dot(a, b, dims):
+        return lax.dot_general(a, b, (dims, ((), ())), preferred_element_type=jnp.float32)
+
+    def compute(part):
+        @pl.loop(0, order // tile)
+        def _(step):
+            x = xbuf[part, at(step), :]
+            zbuf[at(step), :] = dot(x, right[...], ((1,), (1,))).astype(jnp.bfloat16)
+            sig = x.astype(jnp.float32)
+            swish = sig * jax.nn.sigmoid(sig)
+            cot = cbuf[part, at(step), :].astype(jnp.float32)
+            dybuf[at(step), :] = (cot * swish).astype(jnp.bfloat16)
+
+        @pl.loop(0, order // tile)
+        def _(step):
+            dzbuf[at(step), :] = dot(left_t[at(step), :], dybuf[...], ((1,), (0,))).astype(jnp.bfloat16)
+            grad_l[at(step), :] += dot(dybuf[at(step), :], zbuf[...], ((1,), (1,)))
+
+        @pl.loop(0, width // tile)
+        def _(step):
+            grad_r[at(step), :] += dot(dzbuf[:, at(step)], xbuf[part], ((0,), (0,)))
+
+        @pl.loop(0, order // tile)
+        def _(step):
+            y = dot(left[at(step), :], zbuf[...], ((1,), (0,))).astype(jnp.bfloat16).astype(jnp.float32)
+            back = dot(dzbuf[at(step), :], right[...], ((1,), (0,)))
+            sig = xbuf[part, at(step), :].astype(jnp.float32)
+            cot = cbuf[part, at(step), :].astype(jnp.float32)
+            gate = jax.nn.sigmoid(sig)
+            xbuf[part, at(step), :] = (sig + y * (sig * gate)).astype(jnp.bfloat16)
+            dswish = gate * (1.0 + sig * (1.0 - gate))
+            cbuf[part, at(step), :] = (cot * (1.0 + y * dswish) + back).astype(jnp.bfloat16)
+
+    send_in(0)
+    if parts > 1:
+        send_in(1)
+    grad_r[...] = jnp.zeros_like(grad_r)
+    grad_l[...] = jnp.zeros_like(grad_l)
+
+    @pl.loop(0, parts)
+    def _(part):
+        wait_in(part)
+
+        @pl.when(part + 2 < parts)
+        def _():
+            send_in(part + 2)
+
+        compute(part)
+        send_out(part)
+
+    @pl.loop(0, parts)
+    def _(part):
+        wait_in_sent(part)
+        wait_out(part)
+
+
+def shards_by_channel(signal, cotangent, right_factor, left_factor, right_blocks, left_blocks):
+    rows_here, chans, width_two = signal.shape
+    width_one = left_factor.shape[0]
+    peers = lax.axis_size("seq")
+    groups = lax.axis_size("ch")
+    parts = chans // peers
+    right_eff = right_factor * expand(right_blocks, width_two).astype(jnp.bfloat16)
+    left_eff = left_factor * expand(left_blocks, width_one).astype(jnp.bfloat16)
+    xt = signal.transpose(1, 0, 2)
+    ct = cotangent.transpose(1, 0, 2)
+    hbm = pl.BlockSpec(memory_space=pl.ANY)
+    vmem = pl.BlockSpec(memory_space=pltpu.VMEM)
+    mt, gt, right_term, left_term = pl.pallas_call(
+        functools.partial(mix_kernel, peers, parts),
+        out_shape=(
+            jax.ShapeDtypeStruct(xt.shape, jnp.bfloat16),
+            jax.ShapeDtypeStruct(xt.shape, jnp.bfloat16),
+            jax.ShapeDtypeStruct((width_two, width_two), jnp.float32),
+            jax.ShapeDtypeStruct((width_one, width_one), jnp.float32),
+        ),
+        in_specs=[hbm, hbm, vmem, vmem, vmem],
+        out_specs=(hbm, hbm, vmem, vmem),
+        scratch_shapes=[
+            pltpu.VMEM((parts, width_one, width_two), jnp.bfloat16),
+            pltpu.VMEM((parts, width_one, width_two), jnp.bfloat16),
+            pltpu.VMEM((width_one, width_two), jnp.bfloat16),
+            pltpu.VMEM((width_one, width_two), jnp.bfloat16),
+            pltpu.VMEM((width_one, width_two), jnp.bfloat16),
+            pltpu.SemaphoreType.DMA((4, parts, peers)),
+            pltpu.SemaphoreType.DMA((4, parts, peers)),
+            pltpu.SemaphoreType.DMA((4, parts)),
+        ],
+        compiler_params=pltpu.CompilerParams(
+            collective_id=0, has_side_effects=True, vmem_limit_bytes=58 * 2**20
+        ),
+    )(xt, ct, right_eff, left_eff, left_eff.T)
+    mixed = mt.transpose(1, 0, 2)
+    grad_signal = gt.transpose(1, 0, 2)
+    row, col = lax.axis_index("seq"), lax.axis_index("ch")
+
+    def finish(term, blocks, scale):
+        term = lax.psum_scatter(term, "ch", scatter_dimension=1, tiled=True)
+        term = lax.psum_scatter(term, "seq", scatter_dimension=0, tiled=True)
+        mask = expand(blocks, width_two if term.shape[1] * groups == width_two else width_one)
+        mask = lax.dynamic_slice(mask, (row * term.shape[0], col * term.shape[1]), term.shape)
+        return term * mask.astype(jnp.float32) / scale
+
+    grad_right = finish(right_term, right_blocks, math.sqrt(width_one * chans * groups))
+    grad_left = finish(left_term, left_blocks, math.sqrt(width_two * chans * groups))
+    return (mixed, grad_signal, grad_right, grad_left)
+
+
+def shards(signal, *others):
+    rows_here, chans, width_two = signal.shape
+    peers = lax.axis_size("seq")
+    width_one = others[1].shape[0]
+    fits = chans % peers == 0 and rows_here % 16 == 0 and peers > 1
+    if fits and width_one == 1024 and width_two == 1024 and chans // peers <= 4:
+        return shards_by_channel(signal, *others)
+    return shards_by_column(signal, *others)
+
+
 def solution(mesh):
     return jax.shard_map(
         shards,

time: 913 us -> 670 us (0.73); the launches traced: 902 us -> 670 us
  Pallas kernels: 0 us -> 373 us
  local copies, waits for them, and re-layouts: 303 us -> 70.6 us
  blocking collectives: 200 us -> 0 us
  matrix products: 113 us -> 0 us
  other arithmetic: 56.6 us -> 4.88 us
  starting transfers between devices: 10.9 us -> 0.34 us
    pallas_call x0 -> x1, Pallas kernels: none -> 373 us  [shards_by_channel(): pl.pallas_call(functools.partial(mix_kernel, peers, parts), out_shape=(ja...]
    all_to_all x2 -> x0, blocking collectives: 200 us -> none  [the longest x1 100 us: shards(): lax.all_to_all(y_cols, 'seq', split_axis=0, concat_axis=1, tiled=True)]
    reduce_scatter x4, waiting for transfers between devices: 13 us -> 207 us  [the longest x2 153 us: finish(): term = lax.psum_scatter(term, 'ch', scatter_dimension=1, tiled=True)]
    all_to_all x2 -> x0, waiting for transfers between devices: 190 us -> none  [the longest x1 95.2 us: shards(): lax.all_to_all(dz_cols, 'seq', split_axis=0, concat_axis=1, tiled=True)]
    dot_general x6 -> x0, matrix products: 113 us -> none  [the longest x1 40.5 us: shards(): jnp.dot(dz_flat, right_eff, preferred_element_type=jnp.float32)]
    unnamed x15 -> x18, local copies, waits for them, and re-layouts: 108 us -> 34 us
    convert_element_type x4 -> x0, local copies, waits for them, and re-layouts: 64.8 us -> none  [the longest x3 52.9 us: shards(): y_f = y_rows.astype(jnp.float32)]
    all_to_all x4 -> x0, local copies, waits for them, and re-layouts: 52.6 us -> none  [the longest x1 16.8 us: shards(): lax.all_to_all(y_cols, 'seq', split_axis=0, concat_axis=1, tiled=True)]
  transfers between devices with their start and end apart: 6 -> 4, of which waited for: 3 -> 4; matrix products, arithmetic and copies ran while one was open for 19% -> 4% of each run, Pallas kernels for 0% -> 0%
where the time goes in v1:
time: 670 us
  Pallas kernels  373 us (56%)
  waiting for transfers between devices  207 us (31%)
  local copies, waits for them, and re-layouts  70.6 us (11%)
  between operations  13.8 us (2%)
    pallas_call x1, Pallas kernels, shards_by_channel(): pl.pallas_call(functools.partial(mix_kernel, peers, parts), out_shape=(ja...  373 us
    reduce_scatter x2, waiting for transfers between devices, finish(): term = lax.psum_scatter(term, 'ch', scatter_dimension=1, tiled=True)  153 us
    reduce_scatter x2, waiting for transfers between devices, finish(): term = lax.psum_scatter(term, 'seq', scatter_dimension=0, tiled=True)  53.9 us
    unnamed x18, local copies, waits for them, and re-layouts  34 us
    transpose x1, local copies, waits for them, and re-layouts, shards_by_channel(): ct = cotangent.transpose(1, 0, 2)  18.2 us
  transfers between devices with their start and end apart: 4, of which 4 were waited for; matrix products, arithmetic and copies ran while one was open for 4% of the time, Pallas kernels for 0%

profile of v1, /device:TPU:0, one launch (start us, length us, event | category | flops | bytes accessed | tf_op | source)
XLA Modules:
  0.0 669.9 jit_solution(12110296818507912426)
XLA Ops:
  7.2 0.0 reduce-scatter.5.cloned.1.call-start
  7.2 0.6 copy-done
  7.9 0.1 broadcast_bitcast_fusion
  7.9 3.9 copy.13
  11.9 1.8 fusion
  13.6 2.6 copy.15.left
  16.3 0.1 broadcast_bitcast_fusion.1
  16.3 3.9 copy.12
  20.3 3.1 fusion.1
  23.3 3.9 copy.14.right
  27.3 18.2 %copy_bitcast_fusion = (bf16[32,128,1024]{2,1,0:T(8,128)(2,1)}, bf16[32,128,1024]{2,1,0:T(8,128)(2,1)}) fusion(bf16[128,32,1024]{2,1,0:T(8,128)(2,1)} %param.7, bf16[128,32,1024]{2,1,0:T(8,128)(2,1)} %param.6), kind=kLoop, calls=%fused_computation | loop fusion | bytes 33554432 | tf_op jit(solution)/shard_map/transpose | solution.py:270
  45.4 373.0 %shard_map.93 = (bf16[32,128,1024]{2,1,0:T(8,128)(2,1)}, bf16[32,128,1024]{2,1,0:T(8,128)(2,1)}, f32[1024,1024]{1,0:T(8,128)}, f32[1024,1024]{1,0:T(8,128)}) custom-call(bf16[32,128,1024]{2,1,0:T(8,128)(2,1)} %get-tuple-element.17.xt, bf16[32,128,1024]{2,1,0:T(8,128)(2,1)} %get-tuple-element.16.ct, bf16[1024,1024]{1,0:T(8,128)(2,1)} %copy.14.right, ...), custom_call_target="tpu_custom_call" | custom-call | tf_op jit(solution)/shard_map/pallas_call | solution.py:273
  418.4 5.3 copy.16
  423.8 0.0 reduce-scatter.5.cloned.1.call-update
  423.8 0.0 reduce-scatter.9.cloned.1.call-start
  423.8 5.3 copy.17
  429.2 0.0 reduce-scatter.9.cloned.1.call-update
  429.2 0.0 reduce-scatter.7.cloned.1.call-start
  429.3 73.3 %reduce-scatter.5.cloned.1.call-done = f32[1024,256]{0,1:T(8,128)} async-done(((f32[1024,1024]{0,1:T(8,128)}), f32[1024,256]{0,1:T(8,128)}) %reduce-scatter.5.cloned.1.call-update) | async-done | bytes 1048592 | tf_op jit(solution)/shard_map/reduce_scatter | solution.py:302
  502.6 0.0 reduce-scatter.7.cloned.1.call-update
  502.6 0.2 reduce-scatter.11.cloned.1.call-start
  502.8 80.0 %reduce-scatter.9.cloned.1.call-done = f32[1024,256]{0,1:T(8,128)} async-done(((f32[1024,1024]{0,1:T(8,128)}), f32[1024,256]{0,1:T(8,128)}) %reduce-scatter.9.cloned.1.call-update) | async-done | bytes 1048592 | tf_op jit(solution)/shard_map/reduce_scatter | solution.py:302
  582.9 11.5 %copy.18 = bf16[128,32,1024]{2,1,0:T(8,128)(2,1)} copy(bf16[128,32,1024]{2,0,1:T(8,128)(2,1)} %bitcast.21) | data formatting | bytes 16777216
  594.3 11.7 %copy.19 = bf16[128,32,1024]{2,1,0:T(8,128)(2,1)} copy(bf16[128,32,1024]{2,0,1:T(8,128)(2,1)} %bitcast.20) | data formatting | bytes 16777216
  606.1 16.5 %reduce-scatter.7.cloned.1.call-done = f32[128,256]{0,1:T(8,128)} async-done(((f32[1024,256]{0,1:T(8,128)}), f32[128,256]{0,1:T(8,128)}) %reduce-scatter.7.cloned.1.call-update) | async-done | bytes 131088 | tf_op jit(solution)/shard_map/reduce_scatter | solution.py:303
  622.6 0.5 broadcast_in_dim.17
  623.1 0.4 copy-done.3
  623.5 0.8 copy.20
  624.3 37.4 %reduce-scatter.11.cloned.1.call-done = f32[128,256]{0,1:T(8,128)} async-done(((f32[1024,256]{0,1:T(8,128)}), f32[128,256]{0,1:T(8,128)}) %reduce-scatter.11.cloned.1.call-update) | async-done | bytes 131088 | tf_op jit(solution)/shard_map/reduce_scatter | solution.py:303
  661.6 0.5 broadcast_in_dim.19
  662.2 0.4 copy-done.4
  662.6 0.8 copy.21
  (12 shorter events, 0.1 us)
Async XLA Ops:
  7.2 0.7 copy-start
  7.2 495.4 %reduce-scatter.5.cloned.1.call-start = ((), (), s32[]{:S(2)}) async-start(), calls=%async_computation.4 | async-start | bytes 5242880 | tf_op jit(solution)/shard_map/reduce_scatter | solution.py:302
  11.9 4.4 copy-start.5
  13.6 6.6 copy-start.2
  423.8 159.0 %reduce-scatter.9.cloned.1.call-start = ((), (), s32[]{:S(2)}) async-start(), calls=%async_computation.6 | async-start | bytes 5242880 | tf_op jit(solution)/shard_map/reduce_scatter | solution.py:302
  429.2 193.4 %reduce-scatter.7.cloned.1.call-start = ((), (), s32[]{:S(2)}) async-start(), calls=%async_computation.5 | async-start | bytes 1179648 | tf_op jit(solution)/shard_map/reduce_scatter | solution.py:303
  502.6 159.1 %reduce-scatter.11.cloned.1.call-start = ((), (), s32[]{:S(2)}) async-start(), calls=%async_computation.7 | async-start | bytes 1179648 | tf_op jit(solution)/shard_map/reduce_scatter | solution.py:303
  606.1 57.3 %copy-start.1 = (s32[8,8]{1,0:T(8,128)S(1)}, s32[8,8]{1,0:T(8,128)}, u32[]{:S(2)}) copy-start(s32[8,8]{1,0:T(8,128)} %param.11) | copy-start | bytes 772
  622.6 0.9 copy-start.3
  661.6 0.9 copy-start.4
Sparse Core Ops, SparseCore 0:
  423.9 78.6 reduce-scatter.4
  505.5 77.2 reduce-scatter.8
  586.0 36.5 reduce-scatter.6
  625.6 35.9 reduce-scatter.10

commit v2 on v1

--- a/solution.py
+++ b/solution.py
@@ -92,8 +92,10 @@
 
 
 def mix_kernel(
-    peers, parts, xt, ct, right, left, left_t, mt, gt, grad_r, grad_l,
-    xbuf, cbuf, zbuf, dybuf, dzbuf, send_sem, recv_sem, local_sem,
+    peers, groups, parts, scales, right_blocks, left_blocks, xt, ct, right_in, left_in,
+    mt, gt, out_r, out_l, right, left, left_t, grad_r, grad_l,
+    xbuf, cbuf, zbuf, dybuf, dzbuf, pairs, staged, along, summed, across,
+    send_sem, recv_sem, local_sem, pair_sems, along_sems, across_sems,
 ):
     me = lax.axis_index("seq")
     column = lax.axis_index("ch")
@@ -138,7 +140,17 @@
         )
 
     each_peer(greet)
-    pl.semaphore_wait(barrier, peers - 1)
+
+    @pl.loop(1, groups)
+    def _(step):
+        pl.semaphore_signal(
+            barrier,
+            inc=1,
+            device_id=(me, lax.rem(column + step, groups)),
+            device_id_type=pl.DeviceIdType.MESH,
+        )
+
+    pl.semaphore_wait(barrier, peers - 1 + groups - 1)
 
     inputs = ((0, xt, xbuf), (1, ct, cbuf))
     outputs = ((2, mt, xbuf), (3, gt, cbuf))
@@ -235,11 +247,135 @@
             dswish = gate * (1.0 + sig * (1.0 - gate))
             cbuf[part, at(step), :] = (cot * (1.0 + y * dswish) + back).astype(jnp.bfloat16)
 
+    def apply_mask(source, blocks, target):
+        side = source.shape[0] // blocks.shape[0]
+
+        @pl.loop(0, blocks.shape[0])
+        def _(down):
+            here = pl.ds(pl.multiple_of(down * side, side), side)
+            for right_of in range(blocks.shape[1]):
+                there = slice(right_of * side, (right_of + 1) * side)
+                keep = blocks[down, right_of].astype(jnp.float32)
+                target[here, there] = (source[here, there].astype(jnp.float32) * keep).astype(jnp.bfloat16)
+
+    half = peers // 2
+    parity = lax.rem(me, 2)
+    chip = me // 2
+    sibling = me + 1 - 2 * parity
+    cols = width // groups
+    grads = ((0, grad_r), (1, grad_l))
+
+    def between(source, target, sems, going, coming, who):
+        return pltpu.make_async_remote_copy(
+            src_ref=source,
+            dst_ref=target,
+            send_sem=sems.at[0, going[0], going[1]],
+            recv_sem=sems.at[1, coming[0], coming[1]],
+            device_id=who,
+            device_id_type=pl.DeviceIdType.MESH,
+        )
+
+    def pair_copy(kind, grad, block):
+        return between(
+            grad.at[own_rows(2 * block + 1 - parity)], pairs.at[kind, block], pair_sems,
+            (kind, block), (kind, block), (sibling, column),
+        )
+
+    def along_copy(kind, other, slot):
+        return between(
+            staged.at[kind, other], along.at[kind, slot], along_sems, (kind, other), (kind, slot), (me, other)
+        )
+
+    def across_copy(kind, other, slot):
+        return between(
+            summed.at[kind, other], across.at[kind, slot], across_sems,
+            (kind, other), (kind, slot), (2 * other + parity, column),
+        )
+
+    def reduce_over_pairs():
+        @pl.loop(0, half)
+        def _(block):
+            for kind, grad in grads:
+                pair_copy(kind, grad, block).start()
+
+        @pl.loop(0, half)
+        def _(block):
+            for kind, grad in grads:
+                pair_copy(kind, grad, block).wait_recv()
+                for line in range(groups):
+                    there = slice(line * cols, (line + 1) * cols)
+                    staged[kind, line, own_rows(block), :] = (
+                        grad[own_rows(2 * block + parity), there] + pairs[kind, block, :, there]
+                    )
+
+    def send_along():
+        @pl.loop(1, groups)
+        def _(step):
+            for kind in range(2):
+                along_copy(kind, lax.rem(column + step, groups), column).start()
+
+    def finish_sums():
+        @pl.loop(1, groups)
+        def _(step):
+            other = lax.rem(column + step, groups)
+            for kind in range(2):
+                along_copy(kind, other, other).wait_recv()
+
+        @pl.loop(0, half)
+        def _(block):
+            for kind in range(2):
+                total = staged[kind, column, own_rows(block), :]
+                for step in range(1, groups):
+                    total = total + along[kind, lax.rem(column + step, groups), own_rows(block), :]
+                summed[kind, block] = total
+
+        @pl.loop(1, half)
+        def _(step):
+            for kind in range(2):
+                across_copy(kind, lax.rem(chip + step, half), chip).start()
+
+        @pl.loop(1, half)
+        def _(step):
+            other = lax.rem(chip + step, half)
+            for kind in range(2):
+                across_copy(kind, other, other).wait_recv()
+
+        for kind, out, blocks in ((0, out_r, right_blocks), (1, out_l, left_blocks)):
+            side = width // blocks.shape[0]
+            total = summed[kind, chip]
+            for step in range(1, half):
+                total = total + across[kind, lax.rem(chip + step, half)]
+            for right_of in range(cols // side):
+                there = slice(right_of * side, (right_of + 1) * side)
+                keep = blocks[me * rows // side, column * (cols // side) + right_of].astype(jnp.float32)
+                out[:, there] = total[:, there] * keep / scales[kind]
+
+        @pl.loop(0, half)
+        def _(block):
+            for kind, grad in grads:
+                pair_copy(kind, grad, block).wait_send()
+
+        @pl.loop(1, groups)
+        def _(step):
+            for kind in range(2):
+                along_copy(kind, lax.rem(column + step, groups), column).wait_send()
+
+        @pl.loop(1, half)
+        def _(step):
+            for kind in range(2):
+                across_copy(kind, lax.rem(chip + step, half), chip).wait_send()
+
     send_in(0)
     if parts > 1:
         send_in(1)
     grad_r[...] = jnp.zeros_like(grad_r)
     grad_l[...] = jnp.zeros_like(grad_l)
+    apply_mask(right_in, right_blocks, right)
+    apply_mask(left_in, left_blocks, left)
+
+    @pl.loop(0, order // tile)
+    def _(step):
+        left_t[at(step), :] = left[:, at(step)].T
 
     @pl.loop(0, parts)
     def _(part):
@@ -250,7 +386,15 @@
             send_in(part + 2)
 
         compute(part)
-        send_out(part)
+
+        @pl.when(part + 1 < parts)
+        def _():
+            send_out(part)
+
+    reduce_over_pairs()
+    send_along()
+    send_out(parts - 1)
+    finish_sums()
 
     @pl.loop(0, parts)
     def _(part):
@@ -264,57 +408,64 @@
     peers = lax.axis_size("seq")
     groups = lax.axis_size("ch")
     parts = chans // peers
-    right_eff = right_factor * expand(right_blocks, width_two).astype(jnp.bfloat16)
-    left_eff = left_factor * expand(left_blocks, width_one).astype(jnp.bfloat16)
     xt = signal.transpose(1, 0, 2)
     ct = cotangent.transpose(1, 0, 2)
+    half = peers // 2
+    cols = width_two // groups
+    square = (width_one, width_two)
+    block = jax.ShapeDtypeStruct((rows_here, cols), jnp.float32)
+    scales = (math.sqrt(width_one * chans * groups), math.sqrt(width_two * chans * groups))
     hbm = pl.BlockSpec(memory_space=pl.ANY)
     vmem = pl.BlockSpec(memory_space=pltpu.VMEM)
-    mt, gt, right_term, left_term = pl.pallas_call(
-        functools.partial(mix_kernel, peers, parts),
+    smem = pl.BlockSpec(memory_space=pltpu.SMEM)
+    mt, gt, grad_right, grad_left = pl.pallas_call(
+        functools.partial(mix_kernel, peers, groups, parts, scales),
         out_shape=(
             jax.ShapeDtypeStruct(xt.shape, jnp.bfloat16),
             jax.ShapeDtypeStruct(xt.shape, jnp.bfloat16),
-            jax.ShapeDtypeStruct((width_two, width_two), jnp.float32),
-            jax.ShapeDtypeStruct((width_one, width_one), jnp.float32),
+            block,
+            block,
         ),
-        in_specs=[hbm, hbm, vmem, vmem, vmem],
+        in_specs=[smem, smem, hbm, hbm, vmem, vmem],
         out_specs=(hbm, hbm, vmem, vmem),
         scratch_shapes=[
-            pltpu.VMEM((parts, width_one, width_two), jnp.bfloat16),
-            pltpu.VMEM((parts, width_one, width_two), jnp.bfloat16),
-            pltpu.VMEM((width_one, width_two), jnp.bfloat16),
-            pltpu.VMEM((width_one, width_two), jnp.bfloat16),
-            pltpu.VMEM((width_one, width_two), jnp.bfloat16),
+            pltpu.VMEM(square, jnp.bfloat16),
+            pltpu.VMEM(square, jnp.bfloat16),
+            pltpu.VMEM(square, jnp.bfloat16),
+            pltpu.VMEM(square, jnp.float32),
+            pltpu.VMEM(square, jnp.float32),
+            pltpu.VMEM((parts, *square), jnp.bfloat16),
+            pltpu.VMEM((parts, *square), jnp.bfloat16),
+            pltpu.VMEM(square, jnp.bfloat16),
+            pltpu.VMEM(square, jnp.bfloat16),
+            pltpu.VMEM(square, jnp.bfloat16),
+            pltpu.VMEM((2, half, rows_here, width_two), jnp.float32),
+            pltpu.VMEM((2, groups, half * rows_here, cols), jnp.float32),
+            pltpu.VMEM((2, groups, half * rows_here, cols), jnp.float32),
+            pltpu.VMEM((2, half, rows_here, cols), jnp.float32),
+            pltpu.VMEM((2, half, rows_here, cols), jnp.float32),
             pltpu.SemaphoreType.DMA((4, parts, peers)),
             pltpu.SemaphoreType.DMA((4, parts, peers)),
             pltpu.SemaphoreType.DMA((4, parts)),
+            pltpu.SemaphoreType.DMA((2, 2, half)),
+            pltpu.SemaphoreType.DMA((2, 2, groups)),
+            pltpu.SemaphoreType.DMA((2, 2, half)),
         ],
         compiler_params=pltpu.CompilerParams(
-            collective_id=0, has_side_effects=True, vmem_limit_bytes=58 * 2**20
+            collective_id=0, has_side_effects=True, vmem_limit_bytes=60 * 2**20
         ),
-    )(xt, ct, right_eff, left_eff, left_eff.T)
-    mixed = mt.transpose(1, 0, 2)
-    grad_signal = gt.transpose(1, 0, 2)
-    row, col = lax.axis_index("seq"), lax.axis_index("ch")
-
-    def finish(term, blocks, scale):
-        term = lax.psum_scatter(term, "ch", scatter_dimension=1, tiled=True)
-        term = lax.psum_scatter(term, "seq", scatter_dimension=0, tiled=True)
-        mask = expand(blocks, width_two if term.shape[1] * groups == width_two else width_one)
-        mask = lax.dynamic_slice(mask, (row * term.shape[0], col * term.shape[1]), term.shape)
-        return term * mask.astype(jnp.float32) / scale
-
-    grad_right = finish(right_term, right_blocks, math.sqrt(width_one * chans * groups))
-    grad_left = finish(left_term, left_blocks, math.sqrt(width_two * chans * groups))
-    return (mixed, grad_signal, grad_right, grad_left)
+    )(right_blocks, left_blocks, xt, ct, right_factor, left_factor)
+    return (mt.transpose(1, 0, 2), gt.transpose(1, 0, 2), grad_right, grad_left)
 
 
 def shards(signal, *others):
     rows_here, chans, width_two = signal.shape
     peers = lax.axis_size("seq")
     width_one = others[1].shape[0]
-    fits = chans % peers == 0 and rows_here % 16 == 0 and peers > 1
+    sides = (width_two // others[3].shape[0], width_one // others[4].shape[0])
+    fits = chans % peers == 0 and rows_here % 16 == 0 and peers % 2 == 0
+    fits = fits and sides == (128, 128) and rows_here == 128
+    fits = fits and width_two // lax.axis_size("ch") % 128 == 0
     if fits and width_one == 1024 and width_two == 1024 and chans // peers <= 4:
         return shards_by_channel(signal, *others)
     return shards_by_column(signal, *others)

time: 670 us -> 429 us (0.64)
  waiting for transfers between devices: 207 us -> 0 us
  local copies, waits for them, and re-layouts: 70.6 us -> 42.5 us
  between operations: 13.8 us -> 0.64 us
  Pallas kernels: 373 us -> 385 us
    reduce_scatter x4 -> x0, waiting for transfers between devices: 207 us -> none  [the longest x2 153 us: finish(): term = lax.psum_scatter(term, 'ch', scatter_dimension=1, tiled=True)]
    pallas_call x1, Pallas kernels: 373 us -> 385 us  [shards_by_channel(): pl.pallas_call(functools.partial(mix_kernel, peers, groups, parts, scales...]
    pallas_call x2 -> x0, local copies, waits for them, and re-layouts: 10.7 us -> none  [shards_by_channel(): pl.pallas_call(functools.partial(mix_kernel, peers, parts), out_shape=(ja...]
    unnamed x18 -> x8, local copies, waits for them, and re-layouts: 34 us -> 24.3 us
  transfers between devices with their start and end apart: 4 -> 0, of which waited for: 4 -> 0; matrix products, arithmetic and copies ran while one was open for 4% -> 0% of each run, Pallas kernels for 0% -> 0%
where the time goes in v2:
time: 429 us
  Pallas kernels  385 us (90%)
  local copies, waits for them, and re-layouts  42.5 us (10%)
    pallas_call x1, Pallas kernels, shards_by_channel(): pl.pallas_call(functools.partial(mix_kernel, peers, groups, parts, scales...  385 us
    unnamed x8, local copies, waits for them, and re-layouts  24.3 us
    transpose x1, local copies, waits for them, and re-layouts, shards_by_channel(): ct = cotangent.transpose(1, 0, 2)  18.2 us

profile of v2, /device:TPU:0, one launch (start us, length us, event | category | flops | bytes accessed | tf_op | source)
XLA Modules:
  0.0 428.6 jit_solution(6577526954213823562)
XLA Ops:
  0.6 18.2 %copy_bitcast_fusion = (bf16[32,128,1024]{2,1,0:T(8,128)(2,1)}, bf16[32,128,1024]{2,1,0:T(8,128)(2,1)}) fusion(bf16[128,32,1024]{2,1,0:T(8,128)(2,1)} %param.7, bf16[128,32,1024]{2,1,0:T(8,128)(2,1)} %param.6), kind=kLoop, calls=%fused_computation | loop fusion | bytes 33554432 | tf_op jit(solution)/shard_map/transpose | solution.py:412
  18.8 385.5 %shard_map.93 = (bf16[32,128,1024]{2,1,0:T(8,128)(2,1)}, bf16[32,128,1024]{2,1,0:T(8,128)(2,1)}, f32[128,256]{1,0:T(8,128)}, f32[128,256]{1,0:T(8,128)}) custom-call(s32[8,8]{1,0:T(8,128)} %right_blocks.1, s32[8,8]{1,0:T(8,128)} %left_blocks.1, bf16[32,128,1024]{2,1,0:T(8,128)(2,1)} %get-tuple-element.17.xt, bf16[32,128,1024]{2,1,0:T(8,128)(2,1)} %get-tuple-element.16.ct, ...), custom_call_target="tpu_custom_call" | custom-call | tf_op jit(solution)/shard_map/pallas_call | solution.py:421
  404.3 11.5 %copy.12 = bf16[128,32,1024]{2,1,0:T(8,128)(2,1)} copy(bf16[128,32,1024]{2,0,1:T(8,128)(2,1)} %bitcast.7) | data formatting | bytes 16777216
  415.8 0.0 copy-start.1
  415.8 0.0 copy-start
  415.8 11.5 %copy.13 = bf16[128,32,1024]{2,1,0:T(8,128)(2,1)} copy(bf16[128,32,1024]{2,0,1:T(8,128)(2,1)} %bitcast.6) | data formatting | bytes 16777216
  427.3 0.0 copy-done.1
  427.3 0.7 copy.18
  428.0 0.0 copy-done
  428.0 0.7 copy.19
Async XLA Ops:
  415.8 11.5 %copy-start.1 = (f32[128,256]{1,0:T(8,128)S(1)}, f32[128,256]{1,0:T(8,128)}, u32[]{:S(2)}) copy-start(f32[128,256]{1,0:T(8,128)} %get-tuple-element.24) | copy-start | bytes 393220
  415.8 12.2 %copy-start = (f32[128,256]{1,0:T(8,128)S(1)}, f32[128,256]{1,0:T(8,128)}, u32[]{:S(2)}) copy-start(f32[128,256]{1,0:T(8,128)} %get-tuple-element.25) | copy-start | bytes 393220

commit v3 on v2

--- a/solution.py
+++ b/solution.py
@@ -92,15 +92,15 @@
 
 
 def mix_kernel(
-    peers, groups, parts, scales, right_blocks, left_blocks, xt, ct, right_in, left_in,
-    mt, gt, out_r, out_l, right, left, left_t, grad_r, grad_l,
-    xbuf, cbuf, zbuf, dybuf, dzbuf, pairs, staged, along, summed, across,
-    send_sem, recv_sem, local_sem, pair_sems, along_sems, across_sems,
+    peers, groups, parts, scales, right_blocks, left_blocks, signal, cotangent, right_in, left_in,
+    mt, gt, out_r, out_l, right, left, grad_r, grad_l,
+    xbuf, cbuf, zbuf, dybuf, dzbuf, pairs, along, summed, across, slab, turned,
+    send_sem, recv_sem, local_sem, pair_sems, along_sems, across_sems, load_sem,
 ):
     me = lax.axis_index("seq")
     column = lax.axis_index("ch")
-    rows = xt.shape[1]
-    width = xt.shape[2]
+    rows = signal.shape[0]
+    width = signal.shape[2]
     order = left.shape[0]
     tile = 256
 
@@ -133,6 +133,7 @@
             action(lax.rem(me + step, peers))
 
     barrier = pltpu.get_barrier_semaphore()
+    pltpu.make_async_copy(signal.at[:, pl.ds(0, peers), :], slab, load_sem.at[0]).start()
 
     def greet(who):
         pl.semaphore_signal(
@@ -152,37 +153,54 @@
 
     pl.semaphore_wait(barrier, peers - 1 + groups - 1)
 
-    inputs = ((0, xt, xbuf), (1, ct, cbuf))
+    inputs = ((0, signal, xbuf), (1, cotangent, cbuf))
     outputs = ((2, mt, xbuf), (3, gt, cbuf))
 
+    def load(part, kind, source):
+        there = pl.ds(pl.multiple_of(part * peers, peers), peers)
+        return pltpu.make_async_copy(source.at[:, there, :], slab, load_sem.at[kind])
+
+    def start_loads(part):
+        load(part, 0, signal).start()
+
+    def in_copy(kind, part, held, who):
+        return far(kind, part, turned.at[lax.rem(part, 2), kind, who], held.at[part, own_rows(me)], who)
+
+    def own_copy(kind, part, held):
+        return pltpu.make_async_copy(
+            turned.at[lax.rem(part, 2), kind, me], held.at[part, own_rows(me)], local_sem.at[kind, part]
+        )
+
     def send_in(part):
-        def one(who):
-            for kind, source, held in inputs:
-                far(kind, part, source.at[part * peers + who], held.at[part, own_rows(me)], who).start()
-
-        each_peer(one)
         for kind, source, held in inputs:
-            pltpu.make_async_copy(
-                source.at[part * peers + me], held.at[part, own_rows(me)], local_sem.at[kind, part]
-            ).start()
+            load(part, kind, source).wait()
+
+            @pl.loop(0, rows // 16)
+            def _(step):
+                here = pl.ds(pl.multiple_of(step * 16, 16), 16)
+                turned[lax.rem(part, 2), kind, :, here, :] = jnp.swapaxes(slab[here], 0, 1)
+
+            if kind == 0:
+                load(part, 1, cotangent).start()
+
+            each_peer(lambda who: in_copy(kind, part, held, who).start())
+            own_copy(kind, part, held).start()
 
     def wait_in(part):
         def one(who):
             for kind, source, held in inputs:
                 arrived(
-                    kind, part, source.at[part * peers + who], held.at[part, own_rows(who)], who
+                    kind, part, turned.at[lax.rem(part, 2), kind, who], held.at[part, own_rows(who)], who
                 ).wait_recv()
 
         each_peer(one)
         for kind, source, held in inputs:
-            pltpu.make_async_copy(
-                source.at[part * peers + me], held.at[part, own_rows(me)], local_sem.at[kind, part]
-            ).wait()
+            own_copy(kind, part, held).wait()
 
     def wait_in_sent(part):
         def one(who):
             for kind, source, held in inputs:
-                far(kind, part, source.at[part * peers + who], held.at[part, own_rows(me)], who).wait_send()
+                in_copy(kind, part, held, who).wait_send()
 
         each_peer(one)
 
@@ -229,7 +247,7 @@
 
         @pl.loop(0, order // tile)
         def _(step):
-            dzbuf[at(step), :] = dot(left_t[at(step), :], dybuf[...], ((1,), (0,))).astype(jnp.bfloat16)
+            dzbuf[at(step), :] = dot(left[:, at(step)], dybuf[...], ((0,), (0,))).astype(jnp.bfloat16)
             grad_l[at(step), :] += dot(dybuf[at(step), :], zbuf[...], ((1,), (1,)))
 
         @pl.loop(0, width // tile)
@@ -247,8 +265,8 @@
             dswish = gate * (1.0 + sig * (1.0 - gate))
             cbuf[part, at(step), :] = (cot * (1.0 + y * dswish) + back).astype(jnp.bfloat16)
 
-    def apply_mask(source, blocks, target):
-        side = source.shape[0] // blocks.shape[0]
+    def apply_mask(blocks, target):
+        side = target.shape[0] // blocks.shape[0]
 
         @pl.loop(0, blocks.shape[0])
         def _(down):
@@ -256,7 +274,7 @@
             for right_of in range(blocks.shape[1]):
                 there = slice(right_of * side, (right_of + 1) * side)
                 keep = blocks[down, right_of].astype(jnp.float32)
-                target[here, there] = (source[here, there].astype(jnp.float32) * keep).astype(jnp.bfloat16)
+                target[here, there] = (target[here, there].astype(jnp.float32) * keep).astype(jnp.bfloat16)
 
     half = peers // 2
     parity = lax.rem(me, 2)
@@ -281,9 +299,17 @@
             (kind, block), (kind, block), (sibling, column),
         )
 
-    def along_copy(kind, other, slot):
-        return between(
-            staged.at[kind, other], along.at[kind, slot], along_sems, (kind, other), (kind, slot), (me, other)
+    def own_cols(line):
+        return pl.ds(pl.multiple_of(line * cols, cols), cols)
+
+    def along_copy(kind, grad, other, slot, block):
+        return pltpu.make_async_remote_copy(
+            src_ref=grad.at[own_rows(2 * block + parity), own_cols(other)],
+            dst_ref=along.at[kind, slot, own_rows(block)],
+            send_sem=along_sems.at[0, kind, other, block],
+            recv_sem=along_sems.at[1, kind, slot, block],
+            device_id=(me, other),
+            device_id_type=pl.DeviceIdType.MESH,
         )
 
     def across_copy(kind, other, slot):
@@ -302,29 +328,27 @@
         def _(block):
             for kind, grad in grads:
                 pair_copy(kind, grad, block).wait_recv()
-                for line in range(groups):
-                    there = slice(line * cols, (line + 1) * cols)
-                    staged[kind, line, own_rows(block), :] = (
-                        grad[own_rows(2 * block + parity), there] + pairs[kind, block, :, there]
-                    )
+                grad[own_rows(2 * block + parity), :] += pairs[kind, block]
 
     def send_along():
         @pl.loop(1, groups)
         def _(step):
-            for kind in range(2):
-                along_copy(kind, lax.rem(column + step, groups), column).start()
+            for block in range(half):
+                for kind, grad in grads:
+                    along_copy(kind, grad, lax.rem(column + step, groups), column, block).start()
 
     def finish_sums():
         @pl.loop(1, groups)
         def _(step):
             other = lax.rem(column + step, groups)
-            for kind in range(2):
-                along_copy(kind, other, other).wait_recv()
+            for block in range(half):
+                for kind, grad in grads:
+                    along_copy(kind, grad, other, other, block).wait_recv()
 
         @pl.loop(0, half)
         def _(block):
-            for kind in range(2):
-                total = staged[kind, column, own_rows(block), :]
+            for kind, grad in grads:
+                total = grad[own_rows(2 * block + parity), own_cols(column)]
                 for step in range(1, groups):
                     total = total + along[kind, lax.rem(column + step, groups), own_rows(block), :]
                 summed[kind, block] = total
@@ -357,25 +381,34 @@
 
         @pl.loop(1, groups)
         def _(step):
-            for kind in range(2):
-                along_copy(kind, lax.rem(column + step, groups), column).wait_send()
+            for block in range(half):
+                for kind, grad in grads:
+                    along_copy(kind, grad, lax.rem(column + step, groups), column, block).wait_send()
 
         @pl.loop(1, half)
         def _(step):
             for kind in range(2):
                 across_copy(kind, lax.rem(chip + step, half), chip).wait_send()
 
+    fetched = (
+        pltpu.make_async_copy(right_in, right, load_sem.at[2]),
+        pltpu.make_async_copy(left_in, left, load_sem.at[3]),
+    )
     send_in(0)
     if parts > 1:
+        start_loads(1)
+    for copy in fetched:
+        copy.start()
+    if parts > 1:
         send_in(1)
+    if parts > 2:
+        start_loads(2)
+    for copy in fetched:
+        copy.wait()
     grad_r[...] = jnp.zeros_like(grad_r)
     grad_l[...] = jnp.zeros_like(grad_l)
-    apply_mask(right_in, right_blocks, right)
-    apply_mask(left_in, left_blocks, left)
-
-    @pl.loop(0, order // tile)
-    def _(step):
-        left_t[at(step), :] = left[:, at(step)].T
+    apply_mask(right_blocks, right)
+    apply_mask(left_blocks, left)
 
     @pl.loop(0, parts)
     def _(part):
@@ -383,7 +416,12 @@
 
         @pl.when(part + 2 < parts)
         def _():
+            wait_in_sent(part)
             send_in(part + 2)
+
+        @pl.when(part + 3 < parts)
+        def _():
+            start_loads(part + 3)
 
         compute(part)
 
@@ -398,8 +436,28 @@
 
     @pl.loop(0, parts)
     def _(part):
-        wait_in_sent(part)
+        @pl.when(part + 2 >= parts)
+        def _():
+            wait_in_sent(part)
+
         wait_out(part)
+
+
+def turn_kernel(source, target):
+    target[...] = jnp.swapaxes(source[...], 0, 1)
+
+
+def turn_back(array):
+    chans, rows, width = array.shape
+    step = 16
+    return pl.pallas_call(
+        turn_kernel,
+        grid=(rows // step,),
+        out_shape=jax.ShapeDtypeStruct((rows, chans, width), array.dtype),
+        in_specs=[pl.BlockSpec((chans, step, width), lambda place: (0, place, 0))],
+        out_specs=pl.BlockSpec((step, chans, width), lambda place: (place, 0, 0)),
+        compiler_params=pltpu.CompilerParams(vmem_limit_bytes=16 * 2**20),
+    )(array)
 
 
 def shards_by_channel(signal, cotangent, right_factor, left_factor, right_blocks, left_blocks):
@@ -408,8 +466,7 @@
     peers = lax.axis_size("seq")
     groups = lax.axis_size("ch")
     parts = chans // peers
-    xt = signal.transpose(1, 0, 2)
-    ct = cotangent.transpose(1, 0, 2)
+    turned = jax.ShapeDtypeStruct((chans, rows_here, width_two), jnp.bfloat16)
     half = peers // 2
     cols = width_two // groups
     square = (width_one, width_two)
@@ -421,15 +478,14 @@
     mt, gt, grad_right, grad_left = pl.pallas_call(
         functools.partial(mix_kernel, peers, groups, parts, scales),
         out_shape=(
-            jax.ShapeDtypeStruct(xt.shape, jnp.bfloat16),
-            jax.ShapeDtypeStruct(xt.shape, jnp.bfloat16),
+            turned,
+            turned,
             block,
             block,
         ),
-        in_specs=[smem, smem, hbm, hbm, vmem, vmem],
+        in_specs=[smem, smem, hbm, hbm, hbm, hbm],
         out_specs=(hbm, hbm, vmem, vmem),
         scratch_shapes=[
-            pltpu.VMEM(square, jnp.bfloat16),
             pltpu.VMEM(square, jnp.bfloat16),
             pltpu.VMEM(square, jnp.bfloat16),
             pltpu.VMEM(square, jnp.float32),
@@ -441,21 +497,23 @@
             pltpu.VMEM(square, jnp.bfloat16),
             pltpu.VMEM((2, half, rows_here, width_two), jnp.float32),
             pltpu.VMEM((2, groups, half * rows_here, cols), jnp.float32),
-            pltpu.VMEM((2, groups, half * rows_here, cols), jnp.float32),
             pltpu.VMEM((2, half, rows_here, cols), jnp.float32),
             pltpu.VMEM((2, half, rows_here, cols), jnp.float32),
+            pltpu.VMEM((rows_here, peers, width_two), jnp.bfloat16),
+            pltpu.VMEM((2, 2, peers, rows_here, width_two), jnp.bfloat16),
             pltpu.SemaphoreType.DMA((4, parts, peers)),
             pltpu.SemaphoreType.DMA((4, parts, peers)),
             pltpu.SemaphoreType.DMA((4, parts)),
             pltpu.SemaphoreType.DMA((2, 2, half)),
-            pltpu.SemaphoreType.DMA((2, 2, groups)),
+            pltpu.SemaphoreType.DMA((2, 2, groups, half)),
             pltpu.SemaphoreType.DMA((2, 2, half)),
+            pltpu.SemaphoreType.DMA((4,)),
         ],
         compiler_params=pltpu.CompilerParams(
             collective_id=0, has_side_effects=True, vmem_limit_bytes=60 * 2**20
         ),
-    )(right_blocks, left_blocks, xt, ct, right_factor, left_factor)
-    return (mt.transpose(1, 0, 2), gt.transpose(1, 0, 2), grad_right, grad_left)
+    )(right_blocks, left_blocks, signal, cotangent, right_factor, left_factor)
+    return (turn_back(mt), turn_back(gt), grad_right, grad_left)
 
 
 def shards(signal, *others):

time: 429 us -> 402 us (0.937)
  local copies, waits for them, and re-layouts: 42.5 us -> 5.27 us
  Pallas kernels: 385 us -> 396 us
    unnamed x8 -> x10, local copies, waits for them, and re-layouts: 24.3 us -> 5.27 us
    transpose x1 -> x0, local copies, waits for them, and re-layouts: 18.2 us -> none  [shards_by_channel(): ct = cotangent.transpose(1, 0, 2)]
    pallas_call x0 -> x2, Pallas kernels: none -> 11.2 us  [turn_back(): pl.pallas_call(turn_kernel, grid=(rows // step,), out_shape=jax.ShapeDtyp...]
where the time goes in v3:
time: 402 us
  Pallas kernels  396 us (99%)
  local copies, waits for them, and re-layouts  5.27 us (1%)
    pallas_call x1, Pallas kernels, shards_by_channel(): pl.pallas_call(functools.partial(mix_kernel, peers, groups, parts, scales...  385 us
    pallas_call x2, Pallas kernels, turn_back(): pl.pallas_call(turn_kernel, grid=(rows // step,), out_shape=jax.ShapeDtyp...  11.2 us

profile of v3, /device:TPU:0, one launch (start us, length us, event | category | flops | bytes accessed | tf_op | source)
XLA Modules:
  0.0 401.8 jit_solution(1843342024377500530)
XLA Ops:
  0.6 384.7 %shard_map.93 = (bf16[32,128,1024]{2,1,0:T(8,128)(2,1)}, bf16[32,128,1024]{2,1,0:T(8,128)(2,1)}, f32[128,256]{1,0:T(8,128)}, f32[128,256]{1,0:T(8,128)}) custom-call(s32[8,8]{1,0:T(8,128)} %right_blocks.1, s32[8,8]{1,0:T(8,128)} %left_blocks.1, bf16[128,32,1024]{2,1,0:T(8,128)(2,1)} %signal.1, bf16[128,32,1024]{2,1,0:T(8,128)(2,1)} %cotangent.1, ...), custom_call_target="tpu_custom_call" | custom-call | tf_op jit(solution)/shard_map/pallas_call | solution.py:478
  385.3 0.0 copy-start.1
  385.3 3.4 copy-done.1
  388.7 0.0 copy-start
  388.7 5.6 %shard_map.94 = bf16[128,32,1024]{2,1,0:T(8,128)(2,1)} custom-call(bf16[32,128,1024]{2,1,0:T(8,128)(2,1)S(1)} %copy-done.1), custom_call_target="tpu_custom_call" | custom-call | tf_op jit(solution)/shard_map/pallas_call | solution.py:453
  394.3 0.6 copy-done
  394.9 0.0 copy-start.3
  394.9 0.0 copy-start.2
  394.9 5.6 %shard_map.95 = bf16[128,32,1024]{2,1,0:T(8,128)(2,1)} custom-call(bf16[32,128,1024]{2,1,0:T(8,128)(2,1)S(1)} %copy-done), custom_call_target="tpu_custom_call" | custom-call | tf_op jit(solution)/shard_map/pallas_call | solution.py:453
  400.5 0.0 copy-done.3
  400.5 0.7 copy.12
  401.2 0.0 copy-done.2
  401.2 0.7 copy.13
Async XLA Ops:
  385.3 3.4 copy-start.1
  388.7 6.2 %copy-start = (bf16[32,128,1024]{2,1,0:T(8,128)(2,1)S(1)}, bf16[32,128,1024]{2,1,0:T(8,128)(2,1)}, u32[]{:S(2)}) copy-start(bf16[32,128,1024]{2,1,0:T(8,128)(2,1)} %get-tuple-element.9.source) | copy-start | bytes 25165828
  394.9 5.6 %copy-start.3 = (f32[128,256]{1,0:T(8,128)S(1)}, f32[128,256]{1,0:T(8,128)}, u32[]{:S(2)}) copy-start(f32[128,256]{1,0:T(8,128)} %get-tuple-element.18) | copy-start | bytes 393220
  394.9 6.3 %copy-start.2 = (f32[128,256]{1,0:T(8,128)S(1)}, f32[128,256]{1,0:T(8,128)}, u32[]{:S(2)}) copy-start(f32[128,256]{1,0:T(8,128)} %get-tuple-element.19) | copy-start | bytes 393220
